TPU v7x, 32 devices: a whole 2x2x4 slice. The times are simulated.
32 devices in a mesh: dp: 8 (over z, x), tensor: 4 (over y, core).
Axes of the slice: x: 2, y: 2, z: 4, core: 2. Of those that a mesh axis runs over, the one named last changes fastest.
Arguments:
- frames: bfloat16 [2, 32768, 512], P(None, ('dp', 'tensor')), may hold values from -6 to 6
- cotangent: bfloat16 [2, 32768, 512], P(None, ('dp', 'tensor')), may hold values from -6 to 6
- clip_lengths: int32 [2, 32, 4], P(None, 'dp'), may hold values from 1 to 512, 1024 in all within a row
- in_proj: float32 [512, 8, 192], P('dp', 'tensor'), may hold values from -0.25 to 0.25
- out_proj: float32 [8, 64, 512], P('tensor', None, 'dp'), may hold values from -1 to 1
- up_proj: float32 [512, 2048], P('dp', 'tensor'), may hold values from -0.25 to 0.25
- down_proj: float32 [2048, 512], P('tensor', 'dp'), may hold values from -0.125 to 0.125
- small_params: float32 [6, 512], replicated, may hold values from 0.5 to 1.5
- in_first: float32 [512, 8, 192], P('dp', 'tensor'), may hold values from -384 to 384
- in_second: float32 [512, 8, 192], P('dp', 'tensor'), may hold values from 4194.304 to 16777.217
- out_first: float32 [8, 64, 512], P('tensor', None, 'dp'), may hold values from -128 to 128
- out_second: float32 [8, 64, 512], P('tensor', None, 'dp'), may hold values from 589.824 to 2359.296
- up_first: float32 [512, 2048], P('dp', 'tensor'), may hold values from -384 to 384
- up_second: float32 [512, 2048], P('dp', 'tensor'), may hold values from 4096 to 16384
- down_first: float32 [2048, 512], P('tensor', 'dp'), may hold values from -768 to 768
- down_second: float32 [2048, 512], P('tensor', 'dp'), may hold values from 16384 to 65536
- small_first: float32 [6, 512], replicated, may hold values from -1536 to 1536
- small_second: float32 [6, 512], replicated, may hold values from 65536 to 262144
Outputs:
- block_out: bfloat16 [2, 32768, 512], P(None, ('dp', 'tensor'))
- input_grad: bfloat16 [2, 32768, 512], P(None, ('dp', 'tensor'))
- in_new: float32 [512, 8, 192], P('dp', 'tensor')
- in_new_first: float32 [512, 8, 192], P('dp', 'tensor')
- in_new_second: float32 [512, 8, 192], P('dp', 'tensor')
- in_copy: bfloat16 [512, 8, 192], P('dp', 'tensor')
- out_new: float32 [8, 64, 512], P('tensor', None, 'dp')
- out_new_first: float32 [8, 64, 512], P('tensor', None, 'dp')
- out_new_second: float32 [8, 64, 512], P('tensor', None, 'dp')
- out_copy: bfloat16 [8, 64, 512], P('tensor', None, 'dp')
- up_new: float32 [512, 2048], P('dp', 'tensor')
- up_new_first: float32 [512, 2048], P('dp', 'tensor')
- up_new_second: float32 [512, 2048], P('dp', 'tensor')
- up_copy: bfloat16 [512, 2048], P('dp', 'tensor')
- down_new: float32 [2048, 512], P('tensor', 'dp')
- down_new_first: float32 [2048, 512], P('tensor', 'dp')
- down_new_second: float32 [2048, 512], P('tensor', 'dp')
- down_copy: bfloat16 [2048, 512], P('tensor', 'dp')
- small_grad: float32 [6, 512], replicated
- small_new: float32 [6, 512], replicated
- small_new_first: float32 [6, 512], replicated
- small_new_second: float32 [6, 512], replicated
- norms: float32 [2, 10], replicated
Inputs may be any that keep to these rules, and one draw needn't show every extreme that they name: `clip_lengths`: each bucket's 4 runs are whole numbers that sum to 1024; the last run of each bucket is padding.
All inputs are finite; a program needn't handle non-finite values.
Results may differ from a plain program's by a relative error of at most 0.015.
Values may be sent and summed in bfloat16 or wider, within the bound.
A program may use at most 256 MiB of HBM per device.

v0:
```python
import math
import jax
import jax.numpy as jnp
from jax import lax
from jax.sharding import PartitionSpec as P

D = 512
HEAD_DIM = 64
WINDOW = 250
LEN = 1024
CLIPS = 4
MICRO = 2
STEP = 3
beta_first = 0.5
beta_second = 0.5
adam_eps = 1e-06
decay_rate = 0.01
learn_rate = 0.3


def clip_layout(lengths):
    clip_ends = jnp.cumsum(lengths)
    position = jnp.arange(LEN, dtype=jnp.int32)
    clip_of = jnp.sum((position[:, None] >= clip_ends[None, : CLIPS - 1]).astype(jnp.int32), axis=1)
    starts = clip_ends - lengths
    belongs = clip_of[:, None] == jnp.arange(CLIPS, dtype=jnp.int32)[None, :]
    clip_begin = jnp.sum(jnp.where(belongs, starts[None, :], 0), axis=1)
    return (clip_of, position - clip_begin)


def allowed_pairs(clip_of):
    position = jnp.arange(LEN, dtype=jnp.int32)
    causal = position[None, :] <= position[:, None]
    inside = position[:, None] - position[None, :] < WINDOW
    same_clip = clip_of[:, None] == clip_of[None, :]
    return causal & inside & same_clip


def rotate(values_in, offset):
    half_dim = HEAD_DIM // 2
    frequency = jnp.exp(
        jnp.arange(half_dim, dtype=jnp.float32) * (-2.0 * math.log(10000.0) / HEAD_DIM)
    )
    angles = offset.astype(jnp.float32)[:, None] * frequency[None, :]
    cosine = jnp.cos(angles)
    sine = jnp.sin(angles)
    paired = values_in.reshape(values_in.shape[:-1] + (half_dim, 2))
    even_part = paired[..., 0]
    odd_part = paired[..., 1]
    turned = jnp.stack(
        [even_part * cosine - odd_part * sine, even_part * sine + odd_part * cosine], axis=-1
    )
    return turned.reshape(values_in.shape)


def layer_norm(rows, gain, bias):
    centred = rows - jnp.mean(rows, -1, keepdims=True)
    inverse = lax.rsqrt(jnp.mean(centred * centred, -1, keepdims=True) + 1e-05)
    normal = centred * inverse
    return (normal * gain + bias, normal, inverse)


def norm_back(incoming, normal, inverse, gain):
    scaled = incoming * gain
    return inverse * (
        scaled
        - jnp.mean(scaled, -1, keepdims=True)
        - normal * jnp.mean(scaled * normal, -1, keepdims=True)
    )


def gelu_value(values_in):
    return values_in * 0.5 * (1.0 + lax.erf(values_in * (1.0 / math.sqrt(2.0))))


def gelu_slope(values_in):
    cumulative = 0.5 * (1.0 + lax.erf(values_in * (1.0 / math.sqrt(2.0))))
    density = jnp.exp(-0.5 * values_in * values_in) * (1.0 / math.sqrt(2.0 * math.pi))
    return cumulative + values_in * density


def head_scores(queries, keys_rot, clip_of):
    raw = jnp.einsum("qd,kd->qk", queries, keys_rot, preferred_element_type=jnp.float32)
    return jnp.where(allowed_pairs(clip_of), raw * HEAD_DIM ** (-0.5), -1e30)


def attend_forward(head_item):
    head_part, clip_size = head_item
    clip_of, offset = clip_layout(clip_size)
    queries = rotate(head_part[:, 0], offset).astype(jnp.bfloat16)
    keys_rot = rotate(head_part[:, 1], offset).astype(jnp.bfloat16)
    values = head_part[:, 2].astype(jnp.bfloat16)
    scores = head_scores(queries, keys_rot, clip_of)
    top_score = jnp.max(scores, -1, keepdims=True)
    log_total = top_score + jnp.log(jnp.sum(jnp.exp(scores - top_score), -1, keepdims=True))
    attn = jnp.exp(scores - log_total)
    mixed_head = jnp.dot(
        attn.astype(jnp.bfloat16), values, preferred_element_type=jnp.float32
    ).astype(jnp.bfloat16)
    return (jnp.stack([queries, keys_rot, values]), log_total[:, 0], mixed_head)


def attend_back(head_item):
    kept_qkv, log_total, grad_head, clip_size = head_item
    clip_of, offset = clip_layout(clip_size)
    queries = kept_qkv[0]
    keys_rot = kept_qkv[1]
    values = kept_qkv[2]
    attn = jnp.exp(head_scores(queries, keys_rot, clip_of) - log_total[:, None])
    grad_values = jnp.einsum(
        "qk,qd->kd", attn.astype(jnp.bfloat16), grad_head, preferred_element_type=jnp.float32
    )
    grad_attn = jnp.einsum("qd,kd->qk", grad_head, values, preferred_element_type=jnp.float32)
    grad_scores = attn * (grad_attn - jnp.sum(grad_attn * attn, -1, keepdims=True))
    grad_raw = (grad_scores * HEAD_DIM ** (-0.5)).astype(jnp.bfloat16)
    grad_queries = jnp.dot(grad_raw, keys_rot, preferred_element_type=jnp.float32)
    grad_keys = jnp.einsum("qk,qd->kd", grad_raw, queries, preferred_element_type=jnp.float32)
    return jnp.stack(
        [rotate(grad_queries, -offset), rotate(grad_keys, -offset), grad_values], axis=1
    ).astype(jnp.bfloat16)


def split_heads(flat_rows, head_count, item_width):
    blocks = flat_rows.reshape(-1, LEN, head_count, item_width)
    return jnp.moveaxis(blocks, 2, 1).reshape(-1, LEN, item_width)


def merge_heads(head_items, head_count):
    item_width = head_items.shape[-1]
    blocks = head_items.reshape(-1, head_count, LEN, item_width)
    return jnp.moveaxis(blocks, 1, 2).reshape(-1, head_count * item_width)


def reduce_grads(local_grads):
    return (
        lax.psum_scatter(local_grads[0], "dp", scatter_dimension=0, tiled=True),
        lax.psum_scatter(local_grads[1], "dp", scatter_dimension=2, tiled=True),
        lax.psum_scatter(local_grads[2], "dp", scatter_dimension=0, tiled=True),
        lax.psum_scatter(local_grads[3], "dp", scatter_dimension=1, tiled=True),
    )


def on_device(
    frames,
    cotangent,
    clip_lengths,
    in_proj,
    out_proj,
    up_proj,
    down_proj,
    small_params,
    in_first,
    in_second,
    out_first,
    out_second,
    up_first,
    up_second,
    down_first,
    down_second,
    small_first,
    small_second,
):
    rows_here = frames.shape[1]
    own_buckets = rows_here // LEN
    first_bucket = lax.axis_index("tensor") * own_buckets
    copies = (
        in_proj.astype(jnp.bfloat16),
        out_proj.astype(jnp.bfloat16),
        up_proj.astype(jnp.bfloat16),
        down_proj.astype(jnp.bfloat16),
    )
    gathered = (
        lax.all_gather(copies[0], "dp", axis=0, tiled=True),
        lax.all_gather(copies[1], "dp", axis=2, tiled=True),
        lax.all_gather(copies[2], "dp", axis=0, tiled=True),
        lax.all_gather(copies[3], "dp", axis=1, tiled=True),
    )
    in_w, out_w, up_w, down_w = gathered
    head_count = in_w.shape[1]
    in_mat = in_w.reshape(D, -1)
    out_mat = out_w.reshape(-1, D)
    outputs = []
    input_grads = []
    small_terms = jnp.zeros((6, D), jnp.float32)
    owned = None
    for batch_index in range(MICRO):
        group_sizes = clip_lengths[batch_index]
        own_sizes = lax.dynamic_slice_in_dim(group_sizes, first_bucket, own_buckets, 0)
        rows_in = frames[batch_index].astype(jnp.float32)
        normed1, normal1, inverse1 = layer_norm(rows_in, small_params[0], small_params[1])
        enter1 = normed1.astype(jnp.bfloat16)
        enter1_all = lax.all_gather(enter1, "tensor", axis=0, tiled=True)
        projected = jnp.dot(enter1_all, in_mat, preferred_element_type=jnp.float32)
        head_items = split_heads(projected, head_count, 3 * HEAD_DIM).reshape(-1, LEN, 3, HEAD_DIM)
        item_sizes = jnp.repeat(group_sizes, head_count, axis=0)
        kept_qkv, log_totals, mixed_items = lax.map(attend_forward, (head_items, item_sizes))
        mixed_rows = merge_heads(mixed_items, head_count)
        branch = lax.psum_scatter(
            jnp.dot(mixed_rows, out_mat, preferred_element_type=jnp.float32),
            "tensor",
            scatter_dimension=0,
            tiled=True,
        )
        y_first = rows_in + small_params[4] * branch
        normed2, normal2, inverse2 = layer_norm(y_first, small_params[2], small_params[3])
        enter2 = normed2.astype(jnp.bfloat16)
        enter2_all = lax.all_gather(enter2, "tensor", axis=0, tiled=True)
        upval = jnp.dot(enter2_all, up_w, preferred_element_type=jnp.float32)
        act = gelu_value(upval).astype(jnp.bfloat16)
        mlp = lax.psum_scatter(
            jnp.dot(act, down_w, preferred_element_type=jnp.float32).astype(jnp.bfloat16),
            "tensor",
            scatter_dimension=0,
            tiled=True,
        ).astype(jnp.float32)
        outputs.append((y_first + small_params[5] * mlp).astype(jnp.bfloat16))
        clip_of = jax.vmap(lambda length_row: clip_layout(length_row)[0])(own_sizes)
        valid_rows = (clip_of < CLIPS - 1).astype(jnp.float32).reshape(-1)
        grad_y = cotangent[batch_index].astype(jnp.float32) * valid_rows[:, None]
        grad_mlp = (small_params[5] * grad_y).astype(jnp.bfloat16)
        grad_mlp_all = lax.all_gather(grad_mlp, "tensor", axis=0, tiled=True)
        grad_downproj = jnp.einsum(
            "rf,rd->fd", act, grad_mlp_all, preferred_element_type=jnp.float32
        )
        grad_act = jnp.einsum("rd,fd->rf", grad_mlp_all, down_w, preferred_element_type=jnp.float32)
        grad_up = (grad_act * gelu_slope(upval)).astype(jnp.bfloat16)
        grad_upproj = jnp.einsum(
            "rd,rf->df", enter2_all, grad_up, preferred_element_type=jnp.float32
        )
        grad_enter2 = lax.psum_scatter(
            jnp.einsum("rf,df->rd", grad_up, up_w, preferred_element_type=jnp.float32),
            "tensor",
            scatter_dimension=0,
            tiled=True,
        )
        grad_y_first = grad_y + norm_back(grad_enter2, normal2, inverse2, small_params[2])
        grad_branch = (small_params[4] * grad_y_first).astype(jnp.bfloat16)
        grad_branch_all = lax.all_gather(grad_branch, "tensor", axis=0, tiled=True)
        grad_outproj = jnp.einsum(
            "rh,rd->hd", mixed_rows, grad_branch_all, preferred_element_type=jnp.float32
        )
        grad_mixed = jnp.einsum(
            "rd,hd->rh", grad_branch_all, out_mat, preferred_element_type=jnp.float32
        ).astype(jnp.bfloat16)
        grad_items = split_heads(grad_mixed, head_count, HEAD_DIM)
        grad_heads = lax.map(attend_back, (kept_qkv, log_totals, grad_items, item_sizes))
        grad_projected = merge_heads(grad_heads.reshape(-1, LEN, 3 * HEAD_DIM), head_count)
        grad_inproj = jnp.einsum(
            "rd,re->de", enter1_all, grad_projected, preferred_element_type=jnp.float32
        )
        grad_enter1 = lax.psum_scatter(
            jnp.einsum(
                "re,de->rd", grad_projected, in_mat, preferred_element_type=jnp.float32
            ).astype(jnp.bfloat16),
            "tensor",
            scatter_dimension=0,
            tiled=True,
        ).astype(jnp.float32)
        grad_frames = grad_y_first + norm_back(grad_enter1, normal1, inverse1, small_params[0])
        input_grads.append(grad_frames.astype(jnp.bfloat16))
        small_terms = small_terms + jnp.stack(
            [
                jnp.sum(grad_enter1 * normal1, 0),
                jnp.sum(grad_enter1, 0),
                jnp.sum(grad_enter2 * normal2, 0),
                jnp.sum(grad_enter2, 0),
                jnp.sum(grad_y_first * branch, 0),
                jnp.sum(grad_y * mlp, 0),
            ]
        )
        micro_grads = (
            grad_inproj.reshape(in_w.shape),
            grad_outproj.reshape(out_w.shape),
            grad_upproj,
            grad_downproj,
        )
        summed = reduce_grads(micro_grads)
        owned = (
            summed if owned is None else tuple((left + right for left, right in zip(owned, summed)))
        )
    weights_in = (in_proj, out_proj, up_proj, down_proj)
    firsts = (in_first, out_first, up_first, down_first)
    seconds = (in_second, out_second, up_second, down_second)
    own_squares = jnp.stack([jnp.sum(weight * weight) for weight in weights_in])
    small_grad, weight_squares = lax.psum((small_terms, own_squares), ("dp", "tensor"))
    new_firsts = []
    new_seconds = []
    updates = []
    for weight, gradient, first, second in zip(weights_in, owned, firsts, seconds):
        first = beta_first * first + (1.0 - beta_first) * gradient
        second = beta_second * second + (1.0 - beta_second) * gradient * gradient
        update = (
            first
            / (1.0 - beta_first**STEP)
            / (jnp.sqrt(second / (1.0 - beta_second**STEP)) + adam_eps)
            + decay_rate * weight
        )
        new_firsts.append(first)
        new_seconds.append(second)
        updates.append(update)
    update_squares = lax.psum(
        jnp.stack([jnp.sum(update * update) for update in updates]), ("dp", "tensor")
    )
    trust_ratio = jnp.sqrt(weight_squares) * lax.rsqrt(update_squares + 1e-12)
    new_weights = [
        weights_in[index] - learn_rate * trust_ratio[index] * updates[index] for index in range(4)
    ]
    small_first_new = beta_first * small_first + (1.0 - beta_first) * small_grad
    small_second_new = beta_second * small_second + (1.0 - beta_second) * small_grad * small_grad
    small_update = (
        small_first_new
        / (1.0 - beta_first**STEP)
        / (jnp.sqrt(small_second_new / (1.0 - beta_second**STEP)) + adam_eps)
        + decay_rate * small_params
    )
    small_weight_sq = jnp.sum(small_params * small_params, axis=1, keepdims=True)
    small_update_sq = jnp.sum(small_update * small_update, axis=1, keepdims=True)
    small_new = (
        small_params
        - learn_rate * jnp.sqrt(small_weight_sq) * lax.rsqrt(small_update_sq + 1e-12) * small_update
    )
    norms = jnp.stack(
        [
            jnp.concatenate([jnp.sqrt(weight_squares), jnp.sqrt(small_weight_sq).reshape(-1)]),
            jnp.concatenate([jnp.sqrt(update_squares), jnp.sqrt(small_update_sq).reshape(-1)]),
        ]
    )
    block_out = jnp.stack(outputs)
    input_grad = jnp.stack(input_grads)
    return (
        block_out,
        input_grad,
        new_weights[0],
        new_firsts[0],
        new_seconds[0],
        new_weights[0].astype(jnp.bfloat16),
        new_weights[1],
        new_firsts[1],
        new_seconds[1],
        new_weights[1].astype(jnp.bfloat16),
        new_weights[2],
        new_firsts[2],
        new_seconds[2],
        new_weights[2].astype(jnp.bfloat16),
        new_weights[3],
        new_firsts[3],
        new_seconds[3],
        new_weights[3].astype(jnp.bfloat16),
        small_grad,
        small_new,
        small_first_new,
        small_second_new,
        norms,
    )


def solution(mesh):
    return jax.shard_map(
        on_device,
        mesh=mesh,
        in_specs=(
            P(None, ("dp", "tensor"), None),
            P(None, ("dp", "tensor"), None),
            P(None, "dp", None),
            P("dp", "tensor", None),
            P("tensor", None, "dp"),
            P("dp", "tensor"),
            P("tensor", "dp"),
            P(),
            P("dp", "tensor", None),
            P("dp", "tensor", None),
            P("tensor", None, "dp"),
            P("tensor", None, "dp"),
            P("dp", "tensor"),
            P("dp", "tensor"),
            P("tensor", "dp"),
            P("tensor", "dp"),
            P(),
            P(),
        ),
        out_specs=(
            P(None, ("dp", "tensor"), None),
            P(None, ("dp", "tensor"), None),
            P("dp", "tensor", None),
            P("dp", "tensor", None),
            P("dp", "tensor", None),
            P("dp", "tensor", None),
            P("tensor", None, "dp"),
            P("tensor", None, "dp"),
            P("tensor", None, "dp"),
            P("tensor", None, "dp"),
            P("dp", "tensor"),
            P("dp", "tensor"),
            P("dp", "tensor"),
            P("dp", "tensor"),
            P("tensor", "dp"),
            P("tensor", "dp"),
            P("tensor", "dp"),
            P("tensor", "dp"),
            P(),
            P(),
            P(),
            P(),
            P(),
        ),
        check_vma=False,
    )
```

profile of v0, /device:TPU:0, one launch (start us, length us, event | category | flops | bytes accessed | tf_op | source)
XLA Modules:
  0.0 1468.0 jit_solution(3563805246009885565)
XLA Ops:
  14.0 32.6 %all_gather.38 = bf16[2,64,512]{1,0,2:T(2,128)(2,1)S(1)} all-gather(bf16[2,64,64]{1,0,2:T(2,128)(2,1)S(1)} %copy.265), channel_id=1, replica_groups=mesh['dp'=8,'tensor'=4] {'dp'}, dimensions={2}, use_global_device_ids=true | all-gather | bytes 147456 | tf_op jit(solution)/shard_map/all_gather | solution.py:174
  48.0 31.3 %all_gather.37 = bf16[512,2,192]{2,1,0:T(2,128)(2,1)S(1)} all-gather(bf16[64,2,192]{2,1,0:T(2,128)(2,1)S(1)} %get-tuple-element.540), channel_id=1, replica_groups=mesh['dp'=8,'tensor'=4] {'dp'}, dimensions={0}, use_global_device_ids=true | all-gather | bytes 442368 | tf_op jit(solution)/shard_map/all_gather | solution.py:173
  80.4 6.8 fusion.222
  87.2 6.7 fusion.224
  98.3 124.4 %while.48 = (s32[]{:T(128)}, bf16[8,3,1024,64]{2,3,1,0:T(8,128)(2,1)}, f32[8,1024]{1,0:T(8,128)}, bf16[8,1024,64]{1,2,0:T(8,128)(2,1)}, f32[8,1024,3,64]{1,3,2,0...) while((s32[]{:T(128)}, bf16[8,3,1024,64]{2,3,1,0:T(8,128)(2,1)}, f32[8,1024]{1,0:T(8,128)}, ...), condition=%wide.region_8.9_spmd, body=%wide.region_2.8_spmd.sunk | while | flops 284020800 | bytes 21299740 | solution.py:196
  235.7 124.8 %while.49 = (s32[]{:T(128)}, bf16[8,3,1024,64]{2,3,1,0:T(8,128)(2,1)}, f32[8,1024]{1,0:T(8,128)}, bf16[8,1024,64]{1,2,0:T(8,128)(2,1)}, f32[8,1024,3,64]{1,3,2,0...) while((s32[]{:T(128)}, bf16[8,3,1024,64]{2,3,1,0:T(8,128)(2,1)}, f32[8,1024]{1,0:T(8,128)}, ...), condition=%wide.region_21.22_spmd, body=%wide.region_15.21_spmd.sunk | while | flops 284020800 | bytes 21299740 | solution.py:196
  368.7 72.5 %reduce-scatter.19.cloned.1.call-done = f32[1024,512]{1,0:T(8,128)} async-done(((f32[4096,512]{1,0:T(8,128)}), f32[1024,512]{1,0:T(8,128)}) %reduce-scatter.19.cloned.1.call-update) | async-done | bytes 2097168 | tf_op jit(solution)/shard_map/reduce_scatter | solution.py:198
  450.1 31.5 %all_gather.41 = bf16[512,512]{0,1:T(8,128)(2,1)S(1)} all-gather(bf16[512,64]{0,1:T(8,128)(2,1)S(1)} %convert_element_type.346), channel_id=1, replica_groups=mesh['dp'=8,'tensor'=4] {'dp'}, dimensions={1}, use_global_device_ids=true | all-gather | bytes 589824 | tf_op jit(solution)/shard_map/all_gather | solution.py:176
  481.6 31.6 %all_gather.40 = bf16[512,512]{1,0:T(8,128)(2,1)S(1)} all-gather(bf16[64,512]{1,0:T(8,128)(2,1)S(1)} %convert_element_type.344), channel_id=1, replica_groups=mesh['dp'=8,'tensor'=4] {'dp'}, dimensions={0}, use_global_device_ids=true | all-gather | bytes 589824 | tf_op jit(solution)/shard_map/all_gather | solution.py:175
  513.2 7.6 multiply_convert_fusion.3
  520.8 7.6 fusion.149
  536.2 17.3 %all-gather.15.cloned.1.call-done = bf16[4096,512]{1,0:T(8,128)(2,1)} async-done(((bf16[1024,512]{1,0:T(8,128)(2,1)}), bf16[4096,512]{1,0:T(8,128)(2,1)}) %all-gather.15.cloned.1.call-update) | async-done | bytes 4194320 | tf_op jit(solution)/shard_map/all_gather | solution.py:207
  553.5 6.6 multiply_convert_fusion.2
  567.5 7.5 convolution_convert_fusion.3
  575.6 51.9 %reduce-scatter.23.cloned.1.call-done = f32[1024,512]{1,0:T(8,128)} async-done(((f32[4096,512]{1,0:T(8,128)}), f32[1024,512]{1,0:T(8,128)}) %reduce-scatter.23.cloned.1.call-update) | async-done | bytes 2097168 | tf_op jit(solution)/shard_map/reduce_scatter | solution.py:230
  630.7 44.0 %reduce-scatter.21.cloned.1.call-done = bf16[1024,512]{1,0:T(8,128)(2,1)} async-done(((bf16[4096,512]{1,0:T(8,128)(2,1)}), bf16[1024,512]{1,0:T(8,128)(2,1)}) %reduce-scatter.21.cloned.1.call-update) | async-done | bytes 1048592 | tf_op jit(solution)/shard_map/reduce_scatter | solution.py:210
  674.6 47.0 %reduce-scatter.17.cloned.1.call-done = bf16[1024,512]{1,0:T(8,128)(2,1)} async-done(((bf16[4096,512]{1,0:T(8,128)(2,1)}), bf16[1024,512]{1,0:T(8,128)(2,1)}) %reduce-scatter.17.cloned.1.call-update) | async-done | bytes 1048592 | tf_op jit(solution)/shard_map/reduce_scatter | solution.py:210
  721.6 6.3 fusion.201
  728.0 34.6 %all-gather.21.cloned.1.call-done = bf16[4096,512]{1,0:T(8,128)(2,1)} async-done(((bf16[1024,512]{1,0:T(8,128)(2,1)}), bf16[4096,512]{1,0:T(8,128)(2,1)}) %all-gather.21.cloned.1.call-update) | async-done | bytes 4194320 | tf_op jit(solution)/shard_map/all_gather | solution.py:221
  762.5 7.6 fusion.155
  778.0 71.5 %reduce-scatter.27.cloned.1.call-done = f32[1024,512]{1,0:T(8,128)} async-done(((f32[4096,512]{1,0:T(8,128)}), f32[1024,512]{1,0:T(8,128)}) %reduce-scatter.27.cloned.1.call-update) | async-done | bytes 2097168 | tf_op jit(solution)/shard_map/reduce_scatter | solution.py:230
  859.7 6.0 fusion.266
  879.1 14.4 all-gather.19.cloned.1.call-done
  899.1 30.3 %all-gather.23.cloned.1.call-done = bf16[4096,512]{1,0:T(8,128)(2,1)} async-done(((bf16[1024,512]{1,0:T(8,128)(2,1)}), bf16[4096,512]{1,0:T(8,128)(2,1)}) %all-gather.23.cloned.1.call-update) | async-done | bytes 4194320 | tf_op jit(solution)/shard_map/all_gather | solution.py:238
  940.0 100.4 %while.51 = (s32[]{:T(128)}, bf16[8,1024,3,64]{1,3,2,0:T(8,128)(2,1)}, s32[8,4]{1,0:T(8,128)}, bf16[8,3,1024,64]{2,3,1,0:T(8,128)(2,1)}, f32[8,1024]{1,0:T(8,128...) while((s32[]{:T(128)}, bf16[8,1024,3,64]{1,3,2,0:T(8,128)(2,1)}, ...), condition=%wide.region_50.51_spmd, body=%wide.region_45.50_spmd.sunk | while | flops 689820672 | bytes 37543496 | solution.py:246
  1046.2 108.9 %while.50 = (s32[]{:T(128)}, bf16[8,1024,3,64]{1,3,2,0:T(8,128)(2,1)}, s32[8,4]{1,0:T(8,128)}, bf16[8,3,1024,64]{2,3,1,0:T(8,128)(2,1)}, f32[8,1024]{1,0:T(8,128...) while((s32[]{:T(128)}, bf16[8,1024,3,64]{1,3,2,0:T(8,128)(2,1)}, ...), condition=%wide.region_36.37_spmd, body=%wide.region_31.36_spmd.sunk | while | flops 689820672 | bytes 37543496 | solution.py:246
  1181.5 6.2 convolution_convert_fusion
  1201.0 33.4 %reduce-scatter.37.cloned.1.call-done = f32[64,128]{1,0:T(8,128)} async-done(((f32[512,128]{1,0:T(8,128)}), f32[64,128]{1,0:T(8,128)}) %reduce-scatter.37.cloned.1.call-update) | async-done | bytes 32784
  1240.6 60.2 %reduce-scatter.31.cloned.1.call-done = f32[64,2,192]{2,0,1:T(8,128)} async-done(((f32[512,2,192]{2,0,1:T(8,128)}), f32[64,2,192]{2,0,1:T(8,128)}) %reduce-scatter.31.cloned.1.call-update) | async-done | bytes 98320 | tf_op jit(solution)/shard_map/reduce_scatter | solution.py:136
  1308.0 38.9 %reduce-scatter.29.cloned.1.call-done = bf16[1024,512]{1,0:T(8,128)(2,1)} async-done(((bf16[4096,512]{1,0:T(8,128)(2,1)}), bf16[1024,512]{1,0:T(8,128)(2,1)}) %reduce-scatter.29.cloned.1.call-update) | async-done | bytes 1048592 | tf_op jit(solution)/shard_map/reduce_scatter | solution.py:251
  1346.9 47.0 %reduce-scatter.25.cloned.1.call-done = bf16[1024,512]{1,0:T(8,128)(2,1)} async-done(((bf16[4096,512]{1,0:T(8,128)(2,1)}), bf16[1024,512]{1,0:T(8,128)(2,1)}) %reduce-scatter.25.cloned.1.call-update) | async-done | bytes 1048592 | tf_op jit(solution)/shard_map/reduce_scatter | solution.py:251
  1405.2 39.8 %all-reduce = (f32[4]{0:T(128)}, f32[4]{0:T(128)}, f32[6,512]{1,0:T(8,128)}) all-reduce(f32[4]{0:T(128)} %pad_maximum_fusion.8, f32[4]{0:T(128)} %pad_maximum_fusion.7, f32[6,512]{1,0:T(8,128)} %add.375), channel_id=1, replica_groups=mesh['dp'=8,'tensor'=4] {'dp','tensor'}, use_global_device_ids=true, to_apply=%region_71.72 | all-reduce | flops 3080 | bytes 24640 | tf_op jit(solution)/shard_map/psum | solution.py:301
  (1137 shorter events, 648.3 us)
Async XLA Ops:
  7.2 73.2 %all-gather.13.cloned.1.call-start = ((), (), s32[]{:S(2)}) async-start(), calls=%async_computation.16 | async-start | bytes 5242880 | tf_op jit(solution)/shard_map/all_gather | solution.py:192
  13.0 66.8 %copy-start.67 = (s32[2,4,4]{2,1,0:T(4,128)S(1)}, s32[2,4,4]{2,1,0:T(4,128)}, u32[]{:S(2)}) copy-start(s32[2,4,4]{2,1,0:T(4,128)} %param.28) | copy-start | bytes 388
  13.0 74.2 %all-gather.9.cloned.1.call-start = ((), (), s32[]{:S(2)}) async-start(), calls=%async_computation.12 | async-start | bytes 5242880 | tf_op jit(solution)/shard_map/all_gather | solution.py:192
  13.8 354.8 %reduce-scatter.15.cloned.1.call-start = ((), (), s32[]{:S(2)}) async-start(), calls=%async_computation.13 | async-start | bytes 10485760 | tf_op jit(solution)/shard_map/reduce_scatter | solution.py:198
  230.7 210.4 %reduce-scatter.19.cloned.1.call-start = ((), (), s32[]{:S(2)}) async-start(), calls=%async_computation.17 | async-start | bytes 10485760 | tf_op jit(solution)/shard_map/reduce_scatter | solution.py:198
  368.6 72.6 %copy-start.61 = (f32[1,512]{1,0:T(1,128)S(1)}, f32[1,512]{1,0:T(1,128)}, u32[]{:S(2)}) copy-start(f32[1,512]{1,0:T(1,128)} %get-tuple-element.546) | copy-start | bytes 6148
  368.6 144.6 %all-gather.11.cloned.1.call-start = ((), (), s32[]{:S(2)}) async-start(), calls=%async_computation.14 | async-start | bytes 5242880 | tf_op jit(solution)/shard_map/all_gather | solution.py:207
  446.9 73.9 %all-gather.17.cloned.1.call-start = ((), (), s32[]{:S(2)}) async-start(), calls=%async_computation.20 | async-start | bytes 5242880 | tf_op jit(solution)/shard_map/all_gather | solution.py:221
  449.3 104.2 %all-gather.15.cloned.1.call-start = ((), (), s32[]{:S(2)}) async-start(), calls=%async_computation.18 | async-start | bytes 5242880 | tf_op jit(solution)/shard_map/all_gather | solution.py:207
  450.0 177.4 %reduce-scatter.23.cloned.1.call-start = ((), (), s32[]{:S(2)}) async-start(), calls=%async_computation.21 | async-start | bytes 10485760 | tf_op jit(solution)/shard_map/reduce_scatter | solution.py:230
  536.2 138.5 %reduce-scatter.21.cloned.1.call-start = ((), (), s32[]{:S(2)}) async-start(), calls=%async_computation.19 | async-start | bytes 5242880 | tf_op jit(solution)/shard_map/reduce_scatter | solution.py:210
  567.5 154.2 %reduce-scatter.17.cloned.1.call-start = ((), (), s32[]{:S(2)}) async-start(), calls=%async_computation.15 | async-start | bytes 5242880 | tf_op jit(solution)/shard_map/reduce_scatter | solution.py:210
  575.1 187.5 %all-gather.21.cloned.1.call-start = ((), (), s32[]{:S(2)}) async-start(), calls=%async_computation.24 | async-start | bytes 5242880 | tf_op jit(solution)/shard_map/all_gather | solution.py:221
  727.9 121.6 %reduce-scatter.27.cloned.1.call-start = ((), (), s32[]{:S(2)}) async-start(), calls=%async_computation.25 | async-start | bytes 10485760 | tf_op jit(solution)/shard_map/reduce_scatter | solution.py:230
  777.9 71.6 %copy-start.3 = (f32[1024,512]{1,0:T(8,128)S(1)}, f32[1024,512]{1,0:T(8,128)}, u32[]{:S(2)}) copy-start(f32[1024,512]{1,0:T(8,128)} %copy-done.2) | copy-start | bytes 6291460
  777.9 74.9 %copy-start.25 = (bf16[1024,512]{1,0:T(8,128)(2,1)S(1)}, bf16[1024,512]{1,0:T(8,128)(2,1)}, u32[]{:S(2)}) copy-start(bf16[1024,512]{1,0:T(8,128)(2,1)} %reduce-scatter.21.cloned.1.call-done) | copy-start | bytes 3145732
  778.0 115.5 %all-gather.19.cloned.1.call-start = ((), (), s32[]{:S(2)}) async-start(), calls=%async_computation.22 | async-start | bytes 5242880 | tf_op jit(solution)/shard_map/all_gather | solution.py:238
  858.9 70.5 %all-gather.23.cloned.1.call-start = ((), (), s32[]{:S(2)}) async-start(), calls=%async_computation.26 | async-start | bytes 5242880 | tf_op jit(solution)/shard_map/all_gather | solution.py:238
  859.5 333.1 %reduce-scatter.35.cloned.1.call-start = ((), (), s32[]{:S(2)}) async-start(), calls=%async_computation.30 | async-start | bytes 1179648 | tf_op jit(solution)/shard_map/reduce_scatter | solution.py:139
  869.3 326.5 %reduce-scatter.33.cloned.1.call-start = ((), (), s32[]{:S(2)}) async-start(), calls=%async_computation.29 | async-start | bytes 1179648 | tf_op jit(solution)/shard_map/reduce_scatter | solution.py:138
  878.7 355.7 %reduce-scatter.37.cloned.1.call-start = ((), (), s32[]{:S(2)}) async-start(), calls=%async_computation.31 | async-start | bytes 294912
  1046.2 108.9 %copy-start.13 = (bf16[16,8,4,1024]{3,1,2,0:T(8,128)(2,1)S(1)}, bf16[16,8,4,1024]{3,1,2,0:T(8,128)(2,1)}, u32[]{:S(2)}) copy-start(bf16[16,8,4,1024]{3,1,2,0:T(8,128)(2,1)} %copy-done.12) | copy-start | bytes 3145732
  1172.1 128.8 %reduce-scatter.31.cloned.1.call-start = ((), (), s32[]{:S(2)}) async-start(), calls=%async_computation.28 | async-start | bytes 1179648 | tf_op jit(solution)/shard_map/reduce_scatter | solution.py:136
  1181.5 165.5 %reduce-scatter.29.cloned.1.call-start = ((), (), s32[]{:S(2)}) async-start(), calls=%async_computation.27 | async-start | bytes 5242880 | tf_op jit(solution)/shard_map/reduce_scatter | solution.py:251
  1187.8 206.1 %reduce-scatter.25.cloned.1.call-start = ((), (), s32[]{:S(2)}) async-start(), calls=%async_computation.23 | async-start | bytes 5242880 | tf_op jit(solution)/shard_map/reduce_scatter | solution.py:251
  1192.5 108.4 %copy-start.31 = (f32[64,2,192]{2,1,0:T(2,128)S(1)}, f32[64,2,192]{2,1,0:T(2,128)}, u32[]{:S(2)}) copy-start(f32[64,2,192]{2,1,0:T(2,128)} %param.29) | copy-start | bytes 294916
  1198.1 195.8 %copy-start.1 = (bf16[2,1024,512]{2,1,0:T(8,128)(2,1)S(1)}, bf16[2,1024,512]{2,1,0:T(8,128)(2,1)}, u32[]{:S(2)}) copy-start(bf16[2,1024,512]{2,1,0:T(8,128)(2,1)} %param.26) | copy-start | bytes 6291460
  1198.1 195.8 %copy-start.51 = (f32[1024]{0:T(1024)S(1)}, f32[1024]{0:T(1024)}, u32[]{:S(2)}) copy-start(f32[1024]{0:T(1024)} %copy-done.50) | copy-start | bytes 12292
  1198.1 195.8 %copy-start.53 = (f32[1024]{0:T(1024)S(1)}, f32[1024]{0:T(1024)}, u32[]{:S(2)}) copy-start(f32[1024]{0:T(1024)} %copy-done.52) | copy-start | bytes 12292
  1198.1 195.8 %copy-start.57 = (f32[1024]{0:T(1024)S(1)}, f32[1024]{0:T(1024)}, u32[]{:S(2)}) copy-start(f32[1024]{0:T(1024)} %copy-done.56) | copy-start | bytes 12292
  1198.1 195.8 %copy-start.59 = (f32[1024]{0:T(1024)S(1)}, f32[1024]{0:T(1024)}, u32[]{:S(2)}) copy-start(f32[1024]{0:T(1024)} %copy-done.58) | copy-start | bytes 12292
  1346.9 104.4 %copy-start.22 = (bf16[1024,512]{1,0:T(8,128)(2,1)S(1)}, bf16[1024,512]{1,0:T(8,128)(2,1)}, u32[]{:S(2)}) copy-start(bf16[1024,512]{1,0:T(8,128)(2,1)} %reduce-scatter.29.cloned.1.call-done) | copy-start | bytes 3145732
  (59 other events, 271.7 us)
Sparse Core Ops, SparseCore 0:
  13.1 37.1 all-gather.12
  52.5 34.4 all-gather.8
  230.8 72.4 reduce-scatter.14
  368.7 72.3 reduce-scatter.18
  447.0 34.4 all-gather.10
  482.9 34.4 all-gather.16
  519.0 34.4 all-gather.14
  556.1 71.3 reduce-scatter.22
  630.0 44.5 reduce-scatter.20
  677.0 44.5 reduce-scatter.16
  728.0 34.4 all-gather.20
  778.1 71.3 reduce-scatter.26
  859.0 34.4 all-gather.18
  894.9 34.4 all-gather.22
  932.6 64.2 reduce-scatter.34
  1000.2 63.2 reduce-scatter.32
  1172.2 62.0 reduce-scatter.36
  1237.6 63.1 reduce-scatter.30
  1303.4 43.4 reduce-scatter.28
  1349.3 44.5 reduce-scatter.24
where the time goes:
time: 1480 us; the launch traced here: 1470 us
  waiting for transfers between devices  565 us (38%)
  matrix products  269 us (18%)
  local copies, waits for them, and re-layouts  228 us (15%)
  other arithmetic  216 us (15%)
  blocking collectives  167 us (11%)
  between operations  18.1 us (1%)
    reduce_scatter x2, waiting for transfers between devices, on_device(): lax.psum_scatter(jnp.einsum('rf,df->rd', grad_up, up_w, preferred_element...  123 us
    reduce_scatter x2, waiting for transfers between devices, on_device(): lax.psum_scatter(jnp.dot(act, down_w, preferred_element_type=jnp.float32)...  90.9 us
    reduce_scatter x2, waiting for transfers between devices, on_device(): lax.psum_scatter(jnp.einsum('re,de->rd', grad_projected, in_mat, preferre...  85.9 us
    reduce_scatter x2, waiting for transfers between devices, on_device(): lax.psum_scatter(jnp.dot(mixed_rows, out_mat, preferred_element_type=jnp....  72.5 us
    reduce_scatter x1, waiting for transfers between devices, reduce_grads(): lax.psum_scatter(local_grads[0], 'dp', scatter_dimension=0, tiled=True)  60.2 us
    dot_general x32, matrix products, head_scores(): jnp.einsum('qd,kd->qk', queries, keys_rot, preferred_element_type=jnp.flo...  53.3 us
    all_gather x2, waiting for transfers between devices, on_device(): grad_branch_all = lax.all_gather(grad_branch, 'tensor', axis=0, tiled=True)  44.6 us
    psum x1, blocking collectives, on_device(): lax.psum(jnp.stack([jnp.sum(update * update) for update in updates]), ('d...  39.8 us
  transfers between devices with their start and end apart: 20, of which 13 were waited for; matrix products, arithmetic and copies ran while one was open for 34% of the time, Pallas kernels for 0%

commit v1 on v0

--- a/solution.py
+++ b/solution.py
@@ -16,6 +16,22 @@
 adam_eps = 1e-06
 decay_rate = 0.01
 learn_rate = 0.3
+
+
+def ring_gather(x, axis, dim):
+    ways, here, hop = (lax.axis_size(axis), lax.axis_index(axis), x.shape[dim])
+    shape = [n * ways if d == dim else n for d, n in enumerate(x.shape)]
+    full = lax.dynamic_update_slice_in_dim(jnp.zeros(shape, x.dtype), x, here * hop, axis=dim)
+    going_up = going_down = x
+    for far in range(1, ways // 2 + 1):
+        going_up = lax.ppermute(going_up, axis, [(d, (d + 1) % ways) for d in range(ways)])
+        full = lax.dynamic_update_slice_in_dim(full, going_up, (here - far) % ways * hop, axis=dim)
+        if 2 * far < ways:
+            going_down = lax.ppermute(going_down, axis, [(d, (d - 1) % ways) for d in range(ways)])
+            full = lax.dynamic_update_slice_in_dim(
+                full, going_down, (here + far) % ways * hop, axis=dim
+            )
+    return full
 
 
 def clip_layout(lengths):
@@ -218,7 +234,7 @@
         valid_rows = (clip_of < CLIPS - 1).astype(jnp.float32).reshape(-1)
         grad_y = cotangent[batch_index].astype(jnp.float32) * valid_rows[:, None]
         grad_mlp = (small_params[5] * grad_y).astype(jnp.bfloat16)
-        grad_mlp_all = lax.all_gather(grad_mlp, "tensor", axis=0, tiled=True)
+        grad_mlp_all = ring_gather(grad_mlp, "tensor", 0)
         grad_downproj = jnp.einsum(
             "rf,rd->fd", act, grad_mlp_all, preferred_element_type=jnp.float32
         )

time: 1480 us -> 1670 us (1.13)
  local copies, waits for them, and re-layouts: 228 us -> 308 us
  matrix products: 269 us -> 330 us
  waiting for transfers between devices: 565 us -> 611 us
    while x0 -> x128, local copies, waits for them, and re-layouts: none -> 69.1 us
    ppermute x0 -> x6, waiting for transfers between devices: none -> 67.3 us  [the longest x4 67.3 us: ring_gather(): lax.ppermute(going_up, axis, [(d, (d + 1) % ways) for d in range(ways)])]
    reduce_scatter x1, waiting for transfers between devices: 0.02 us -> 64.2 us  [reduce_grads(): lax.psum_scatter(local_grads[3], 'dp', scatter_dimension=1, tiled=True)]
    dot_general x16, matrix products: 23 us -> 57.7 us  [attend_forward(): jnp.dot(attn.astype(jnp.bfloat16), values, preferred_element_type=jnp.flo...]
    all_gather x2 -> x0, waiting for transfers between devices: 34.6 us -> none  [on_device(): grad_mlp_all = lax.all_gather(grad_mlp, 'tensor', axis=0, tiled=True)]
    dot_general x16, matrix products: 27.5 us -> 52.1 us  [attend_back(): jnp.einsum('qd,kd->qk', grad_head, values, preferred_element_type=jnp.flo...]
    all_gather x2, waiting for transfers between devices: 44.6 us -> 23.8 us  [on_device(): grad_branch_all = lax.all_gather(grad_branch, 'tensor', axis=0, tiled=True)]
    all_gather x2, waiting for transfers between devices: 17.3 us -> 0.02 us  [on_device(): enter2_all = lax.all_gather(enter2, 'tensor', axis=0, tiled=True)]
  transfers between devices with their start and end apart: 20 -> 24, of which waited for: 13 -> 14; matrix products, arithmetic and copies ran while one was open for 34% -> 42% of each run, Pallas kernels for 0% -> 0%
where the time goes in v1:
time: 1670 us; the launch traced here: 1650 us
  waiting for transfers between devices  611 us (37%)
  matrix products  330 us (20%)
  local copies, waits for them, and re-layouts  308 us (18%)
  other arithmetic  206 us (12%)
  blocking collectives  167 us (10%)
  between operations  18.2 us (1%)
    reduce_scatter x2, waiting for transfers between devices, on_device(): lax.psum_scatter(jnp.einsum('rf,df->rd', grad_up, up_w, preferred_element...  115 us
    reduce_scatter x2, waiting for transfers between devices, on_device(): lax.psum_scatter(jnp.einsum('re,de->rd', grad_projected, in_mat, preferre...  86.1 us
    reduce_scatter x2, waiting for transfers between devices, on_device(): lax.psum_scatter(jnp.dot(act, down_w, preferred_element_type=jnp.float32)...  83.9 us
    reduce_scatter x2, waiting for transfers between devices, on_device(): lax.psum_scatter(jnp.dot(mixed_rows, out_mat, preferred_element_type=jnp....  72.3 us
    while x128, local copies, waits for them, and re-layouts  69.1 us
    ppermute x4, waiting for transfers between devices, ring_gather(): lax.ppermute(going_up, axis, [(d, (d + 1) % ways) for d in range(ways)])  67.3 us
    reduce_scatter x1, waiting for transfers between devices, reduce_grads(): lax.psum_scatter(local_grads[3], 'dp', scatter_dimension=1, tiled=True)  64.2 us
    reduce_scatter x1, waiting for transfers between devices, reduce_grads(): lax.psum_scatter(local_grads[0], 'dp', scatter_dimension=0, tiled=True)  60 us
  transfers between devices with their start and end apart: 24, of which 14 were waited for; matrix products, arithmetic and copies ran while one was open for 42% of the time, Pallas kernels for 0%

profile of v1, /device:TPU:0, one launch (start us, length us, event | category | flops | bytes accessed | tf_op | source)
XLA Modules:
  0.0 1649.4 jit_solution(2800905554426025713)
XLA Ops:
  15.4 33.1 %all_gather.31 = bf16[512,2,192]{2,1,0:T(2,128)(2,1)S(1)} all-gather(bf16[64,2,192]{2,1,0:T(2,128)(2,1)S(1)} %get-tuple-element.543), channel_id=1, replica_groups=mesh['dp'=8,'tensor'=4] {'dp'}, dimensions={0}, use_global_device_ids=true | all-gather | bytes 442368 | tf_op jit(solution)/shard_map/all_gather | solution.py:189
  49.7 30.7 %all_gather.32 = bf16[2,64,512]{1,0,2:T(2,128)(2,1)S(1)} all-gather(bf16[2,64,64]{1,0,2:T(2,128)(2,1)S(1)} %copy.265), channel_id=1, replica_groups=mesh['dp'=8,'tensor'=4] {'dp'}, dimensions={2}, use_global_device_ids=true | all-gather | bytes 147456 | tf_op jit(solution)/shard_map/all_gather | solution.py:190
  81.3 6.7 fusion.222
  92.3 158.1 %while.49 = (s32[]{:T(128)}, bf16[8,3,1024,64]{2,3,1,0:T(8,128)(2,1)}, f32[8,1024]{1,0:T(8,128)}, bf16[8,1024,64]{1,2,0:T(8,128)(2,1)}, f32[8,1024,3,64]{1,3,2,0...) while((s32[]{:T(128)}, bf16[8,3,1024,64]{2,3,1,0:T(8,128)(2,1)}, f32[8,1024]{1,0:T(8,128)}, ...), condition=%wide.region_21.22_spmd, body=%wide.region_15.21_spmd.sunk | while | flops 284020800 | bytes 38076984 | solution.py:212
  259.4 6.8 fusion.224
  270.3 147.3 %while.48 = (s32[]{:T(128)}, bf16[8,3,1024,64]{2,3,1,0:T(8,128)(2,1)}, f32[8,1024]{1,0:T(8,128)}, bf16[8,1024,64]{1,2,0:T(8,128)(2,1)}, f32[8,1024,3,64]{1,3,2,0...) while((s32[]{:T(128)}, bf16[8,3,1024,64]{2,3,1,0:T(8,128)(2,1)}, f32[8,1024]{1,0:T(8,128)}, ...), condition=%wide.region_8.9_spmd, body=%wide.region_2.8_spmd.sunk | while | flops 284020800 | bytes 38078064 | solution.py:212
  425.7 72.3 %reduce-scatter.15.cloned.1.call-done = f32[1024,512]{1,0:T(8,128)} async-done(((f32[4096,512]{1,0:T(8,128)}), f32[1024,512]{1,0:T(8,128)}) %reduce-scatter.15.cloned.1.call-update) | async-done | bytes 2097168 | tf_op jit(solution)/shard_map/reduce_scatter | solution.py:214
  516.0 34.9 %collective-permute-done = bf16[1024,512]{1,0:T(8,128)(2,1)} collective-permute-done((bf16[1024,512]{1,0:T(8,128)(2,1)}, bf16[1024,512]{1,0:T(8,128)(2,1)}, u32[]{:S(2)}, u32[]{:S(2)}) %collective-permute-start) | collective-permute-done | bytes 1048608 | tf_op jit(solution)/shard_map/ppermute | solution.py:27
  550.9 31.3 %collective-permute-done.3 = bf16[1024,512]{1,0:T(8,128)(2,1)S(1)} collective-permute-done((bf16[1024,512]{1,0:T(8,128)(2,1)}, bf16[1024,512]{1,0:T(8,128)(2,1)S(1)}, u32[]{:S(2)}, u32[]{:S(2)}) %collective-permute-start.3) | collective-permute-done | bytes 1048608 | tf_op jit(solution)/shard_map/ppermute | solution.py:27
  582.2 31.4 %all_gather.34 = bf16[512,512]{1,0:T(8,128)(2,1)S(1)} all-gather(bf16[64,512]{1,0:T(8,128)(2,1)S(1)} %convert_element_type.344), channel_id=1, replica_groups=mesh['dp'=8,'tensor'=4] {'dp'}, dimensions={0}, use_global_device_ids=true | all-gather | bytes 589824 | tf_op jit(solution)/shard_map/all_gather | solution.py:191
  627.2 6.7 multiply_convert_fusion.2
  638.2 6.6 multiply_convert_fusion.3
  652.5 64.2 %reduce-scatter.35.cloned.1.call-done = f32[512,64]{0,1:T(8,128)} async-done(((f32[512,512]{0,1:T(8,128)}), f32[512,64]{0,1:T(8,128)}) %reduce-scatter.35.cloned.1.call-update) | async-done | bytes 131088 | tf_op jit(solution)/shard_map/reduce_scatter | solution.py:155
  719.0 31.7 %all_gather.35 = bf16[512,512]{0,1:T(8,128)(2,1)S(1)} all-gather(bf16[512,64]{0,1:T(8,128)(2,1)S(1)} %get-tuple-element.544), channel_id=1, replica_groups=mesh['dp'=8,'tensor'=4] {'dp'}, dimensions={1}, use_global_device_ids=true | all-gather | bytes 589824 | tf_op jit(solution)/shard_map/all_gather | solution.py:192
  750.7 7.6 fusion.149
  766.3 7.7 fusion.155
  782.4 6.6 convolution_convert_fusion.2
  789.4 6.5 convolution_convert_fusion.3
  795.9 40.5 %reduce-scatter.23.cloned.1.call-done = f32[1024,512]{1,0:T(8,128)} async-done(((f32[4096,512]{1,0:T(8,128)}), f32[1024,512]{1,0:T(8,128)}) %reduce-scatter.23.cloned.1.call-update) | async-done | bytes 2097168 | tf_op jit(solution)/shard_map/reduce_scatter | solution.py:246
  836.5 74.0 %reduce-scatter.27.cloned.1.call-done = f32[1024,512]{1,0:T(8,128)} async-done(((f32[4096,512]{1,0:T(8,128)}), f32[1024,512]{1,0:T(8,128)}) %reduce-scatter.27.cloned.1.call-update) | async-done | bytes 2097168 | tf_op jit(solution)/shard_map/reduce_scatter | solution.py:246
  914.9 42.6 %reduce-scatter.21.cloned.1.call-done = bf16[1024,512]{1,0:T(8,128)(2,1)} async-done(((bf16[4096,512]{1,0:T(8,128)(2,1)}), bf16[1024,512]{1,0:T(8,128)(2,1)}) %reduce-scatter.21.cloned.1.call-update) | async-done | bytes 1048592 | tf_op jit(solution)/shard_map/reduce_scatter | solution.py:226
  963.3 41.3 %reduce-scatter.17.cloned.1.call-done = bf16[1024,512]{1,0:T(8,128)(2,1)} async-done(((bf16[4096,512]{1,0:T(8,128)(2,1)}), bf16[1024,512]{1,0:T(8,128)(2,1)}) %reduce-scatter.17.cloned.1.call-update) | async-done | bytes 1048592 | tf_op jit(solution)/shard_map/reduce_scatter | solution.py:226
  1004.6 6.4 fusion.201
  1023.8 23.8 %all-gather.15.cloned.1.call-done = bf16[4096,512]{1,0:T(8,128)(2,1)} async-done(((bf16[1024,512]{1,0:T(8,128)(2,1)}), bf16[4096,512]{1,0:T(8,128)(2,1)}) %all-gather.15.cloned.1.call-update) | async-done | bytes 4194320 | tf_op jit(solution)/shard_map/all_gather | solution.py:254
  1057.0 128.5 %while.50 = (s32[]{:T(128)}, bf16[8,1024,3,64]{1,3,2,0:T(8,128)(2,1)}, s32[8,4]{1,0:T(8,128)S(1)}, bf16[8,3,1024,64]{2,3,1,0:T(8,128)(2,1)}, f32[8,1024]{1,0:T(8...) while((s32[]{:T(128)}, bf16[8,1024,3,64]{1,3,2,0:T(8,128)(2,1)}, ...), condition=%wide.region_36.37_spmd, body=%wide.region_31.36_spmd.sunk | while | flops 689820672 | bytes 71097976 | solution.py:262
  1195.0 139.3 %while.51 = (s32[]{:T(128)}, bf16[8,1024,3,64]{1,3,2,0:T(8,128)(2,1)}, s32[8,4]{1,0:T(8,128)}, bf16[8,3,1024,64]{2,3,1,0:T(8,128)(2,1)}, f32[8,1024]{1,0:T(8,128...) while((s32[]{:T(128)}, bf16[8,1024,3,64]{1,3,2,0:T(8,128)(2,1)}, ...), condition=%wide.region_50.51_spmd, body=%wide.region_45.50_spmd.sunk | while | flops 689820672 | bytes 71097976 | solution.py:262
  1361.5 6.2 convolution_convert_fusion.1
  1378.4 36.9 %reduce-scatter.37.cloned.1.call-done = f32[64,128]{1,0:T(8,128)} async-done(((f32[512,128]{1,0:T(8,128)}), f32[64,128]{1,0:T(8,128)}) %reduce-scatter.37.cloned.1.call-update) | async-done | bytes 32784
  1421.8 60.0 %reduce-scatter.31.cloned.1.call-done = f32[64,2,192]{2,0,1:T(8,128)} async-done(((f32[512,2,192]{2,0,1:T(8,128)}), f32[64,2,192]{2,0,1:T(8,128)}) %reduce-scatter.31.cloned.1.call-update) | async-done | bytes 98320 | tf_op jit(solution)/shard_map/reduce_scatter | solution.py:152
  1488.8 39.1 %reduce-scatter.25.cloned.1.call-done = bf16[1024,512]{1,0:T(8,128)(2,1)} async-done(((bf16[4096,512]{1,0:T(8,128)(2,1)}), bf16[1024,512]{1,0:T(8,128)(2,1)}) %reduce-scatter.25.cloned.1.call-update) | async-done | bytes 1048592 | tf_op jit(solution)/shard_map/reduce_scatter | solution.py:267
  1527.9 47.0 %reduce-scatter.29.cloned.1.call-done = bf16[1024,512]{1,0:T(8,128)(2,1)} async-done(((bf16[4096,512]{1,0:T(8,128)(2,1)}), bf16[1024,512]{1,0:T(8,128)(2,1)}) %reduce-scatter.29.cloned.1.call-update) | async-done | bytes 1048592 | tf_op jit(solution)/shard_map/reduce_scatter | solution.py:267
  1586.2 40.0 %all-reduce = (f32[4]{0:T(128)}, f32[4]{0:T(128)}, f32[6,512]{1,0:T(8,128)}) all-reduce(f32[4]{0:T(128)} %pad_maximum_fusion.8, f32[4]{0:T(128)} %pad_maximum_fusion.7, f32[6,512]{1,0:T(8,128)} %add.418), channel_id=1, replica_groups=mesh['dp'=8,'tensor'=4] {'dp','tensor'}, use_global_device_ids=true, to_apply=%region_71.72 | all-reduce | flops 3080 | bytes 24640 | tf_op jit(solution)/shard_map/psum | solution.py:317
  (1276 shorter events, 784.5 us)
Async XLA Ops:
  7.2 74.1 %all-gather.11.cloned.1.call-start = ((), (), s32[]{:S(2)}) async-start(), calls=%async_computation.16 | async-start | bytes 5242880 | tf_op jit(solution)/shard_map/all_gather | solution.py:208
  13.8 244.9 %all-gather.7.cloned.1.call-start = ((), (), s32[]{:S(2)}) async-start(), calls=%async_computation.12 | async-start | bytes 5242880 | tf_op jit(solution)/shard_map/all_gather | solution.py:208
  14.5 411.1 %reduce-scatter.19.cloned.1.call-start = ((), (), s32[]{:S(2)}) async-start(), calls=%async_computation.17 | async-start | bytes 10485760 | tf_op jit(solution)/shard_map/reduce_scatter | solution.py:214
  258.4 239.6 %reduce-scatter.15.cloned.1.call-start = ((), (), s32[]{:S(2)}) async-start(), calls=%async_computation.13 | async-start | bytes 10485760 | tf_op jit(solution)/shard_map/reduce_scatter | solution.py:214
  425.6 201.6 %all-gather.13.cloned.1.call-start = ((), (), s32[]{:S(2)}) async-start(), calls=%async_computation.18 | async-start | bytes 5242880 | tf_op jit(solution)/shard_map/all_gather | solution.py:223
  503.7 134.6 %all-gather.9.cloned.1.call-start = ((), (), s32[]{:S(2)}) async-start(), calls=%async_computation.14 | async-start | bytes 5242880 | tf_op jit(solution)/shard_map/all_gather | solution.py:223
  504.2 212.5 %reduce-scatter.35.cloned.1.call-start = ((), (), s32[]{:S(2)}) async-start(), calls=%async_computation.28 | async-start | bytes 1179648 | tf_op jit(solution)/shard_map/reduce_scatter | solution.py:155
  509.2 41.7 %collective-permute-start = (bf16[1024,512]{1,0:T(8,128)(2,1)}, bf16[1024,512]{1,0:T(8,128)(2,1)}, u32[]{:S(2)}, u32[]{:S(2)}) collective-permute-start(bf16[1024,512]{1,0:T(8,128)(2,1)} %get-tuple-element.469), channel_id=1, source_target_pairs={{0,1},{1,2},{2,3},{3,0},{4,5},{5,6},{6,7},{7,4},{8,9},{9,10},{10,1... | collective-permute-start | bytes 3145736 | tf_op jit(solution)/shard_map/ppermute | solution.py:27
  513.3 68.9 %collective-permute-start.3 = (bf16[1024,512]{1,0:T(8,128)(2,1)}, bf16[1024,512]{1,0:T(8,128)(2,1)S(1)}, u32[]{:S(2)}, u32[]{:S(2)}) collective-permute-start(bf16[1024,512]{1,0:T(8,128)(2,1)} %get-tuple-element.471), channel_id=1, source_target_pairs={{0,1},{1,2},{2,3},{3,0},{4,5},{5,6},{6,7},{7,4},{8,9},{9,10},{10,1... | collective-permute-start | bytes 3145736 | tf_op jit(solution)/shard_map/ppermute | solution.py:27
  514.2 102.8 %collective-permute-start.1 = (bf16[1024,512]{1,0:T(8,128)(2,1)}, bf16[1024,512]{1,0:T(8,128)(2,1)}, u32[]{:S(2)}, u32[]{:S(2)}) collective-permute-start(bf16[1024,512]{1,0:T(8,128)(2,1)} %get-tuple-element.469), channel_id=1, source_target_pairs={{0,3},{1,0},{2,1},{3,2},{4,7},{5,4},{6,5},{7,6},{8,11},{9,8},{10,9... | collective-permute-start | bytes 3145736 | tf_op jit(solution)/shard_map/ppermute | solution.py:30
  515.6 103.7 %collective-permute-start.4 = (bf16[1024,512]{1,0:T(8,128)(2,1)}, bf16[1024,512]{1,0:T(8,128)(2,1)}, u32[]{:S(2)}, u32[]{:S(2)}) collective-permute-start(bf16[1024,512]{1,0:T(8,128)(2,1)} %get-tuple-element.471), channel_id=1, source_target_pairs={{0,3},{1,0},{2,1},{3,2},{4,7},{5,4},{6,5},{7,6},{8,11},{9,8},{10,9... | collective-permute-start | bytes 3145736 | tf_op jit(solution)/shard_map/ppermute | solution.py:30
  550.9 70.6 %collective-permute-start.2 = (bf16[1024,512]{1,0:T(8,128)(2,1)}, bf16[1024,512]{1,0:T(8,128)(2,1)}, u32[]{:S(2)}, u32[]{:S(2)}) collective-permute-start(bf16[1024,512]{1,0:T(8,128)(2,1)} %collective-permute-done), channel_id=1, source_target_pairs={{0,1},{1,2},{2,3},{3,0},{4,5},{5,6},{6,7},{7,4},{8,9},{9,10},{10,1... | collective-permute-start | bytes 3145736 | tf_op jit(solution)/shard_map/ppermute | solution.py:27
  582.2 42.7 %collective-permute-start.5 = (bf16[1024,512]{1,0:T(8,128)(2,1)S(1)}, bf16[1024,512]{1,0:T(8,128)(2,1)}, u32[]{:S(2)}, u32[]{:S(2)}) collective-permute-start(bf16[1024,512]{1,0:T(8,128)(2,1)S(1)} %collective-permute-done.3), channel_id=1, source_target_pairs={{0,1},{1,2},{2,3},{3,0},{4,5},{5,6},{6,7},{7,4},{8,9},{9,10},{10,1... | collective-permute-start | bytes 3145736 | tf_op jit(solution)/shard_map/ppermute | solution.py:27
  652.4 184.0 %reduce-scatter.23.cloned.1.call-start = ((), (), s32[]{:S(2)}) async-start(), calls=%async_computation.20 | async-start | bytes 10485760 | tf_op jit(solution)/shard_map/reduce_scatter | solution.py:246
  766.2 144.3 %reduce-scatter.27.cloned.1.call-start = ((), (), s32[]{:S(2)}) async-start(), calls=%async_computation.23 | async-start | bytes 10485760 | tf_op jit(solution)/shard_map/reduce_scatter | solution.py:246
  782.4 175.0 %reduce-scatter.21.cloned.1.call-start = ((), (), s32[]{:S(2)}) async-start(), calls=%async_computation.19 | async-start | bytes 5242880 | tf_op jit(solution)/shard_map/reduce_scatter | solution.py:226
  789.1 215.5 %reduce-scatter.17.cloned.1.call-start = ((), (), s32[]{:S(2)}) async-start(), calls=%async_computation.15 | async-start | bytes 5242880 | tf_op jit(solution)/shard_map/reduce_scatter | solution.py:226
  795.8 114.6 %copy-start.9 = (f32[1024,512]{1,0:T(8,128)S(1)}, f32[1024,512]{1,0:T(8,128)}, u32[]{:S(2)}) copy-start(f32[1024,512]{1,0:T(8,128)} %copy-done.8) | copy-start | bytes 6291460
  795.9 251.8 %all-gather.15.cloned.1.call-start = ((), (), s32[]{:S(2)}) async-start(), calls=%async_computation.21 | async-start | bytes 5242880 | tf_op jit(solution)/shard_map/all_gather | solution.py:254
  1013.0 172.5 %all-gather.17.cloned.1.call-start = ((), (), s32[]{:S(2)}) async-start(), calls=%async_computation.24 | async-start | bytes 5242880 | tf_op jit(solution)/shard_map/all_gather | solution.py:254
  1013.8 358.5 %reduce-scatter.33.cloned.1.call-start = ((), (), s32[]{:S(2)}) async-start(), calls=%async_computation.27 | async-start | bytes 1179648 | tf_op jit(solution)/shard_map/reduce_scatter | solution.py:154
  1023.3 392.0 %reduce-scatter.37.cloned.1.call-start = ((), (), s32[]{:S(2)}) async-start(), calls=%async_computation.29 | async-start | bytes 294912
  1353.1 128.8 %reduce-scatter.31.cloned.1.call-start = ((), (), s32[]{:S(2)}) async-start(), calls=%async_computation.26 | async-start | bytes 1179648 | tf_op jit(solution)/shard_map/reduce_scatter | solution.py:152
  1361.5 166.4 %reduce-scatter.25.cloned.1.call-start = ((), (), s32[]{:S(2)}) async-start(), calls=%async_computation.22 | async-start | bytes 5242880 | tf_op jit(solution)/shard_map/reduce_scatter | solution.py:267
  1367.8 207.1 %reduce-scatter.29.cloned.1.call-start = ((), (), s32[]{:S(2)}) async-start(), calls=%async_computation.25 | async-start | bytes 5242880 | tf_op jit(solution)/shard_map/reduce_scatter | solution.py:267
  1372.2 109.6 %copy-start.38 = (f32[64,2,192]{2,1,0:T(2,128)S(1)}, f32[64,2,192]{2,1,0:T(2,128)}, u32[]{:S(2)}) copy-start(f32[64,2,192]{2,1,0:T(2,128)} %param.29) | copy-start | bytes 294916
  1375.5 199.4 %copy-start.7 = (bf16[2,1024,512]{2,1,0:T(8,128)(2,1)S(1)}, bf16[2,1024,512]{2,1,0:T(8,128)(2,1)}, u32[]{:S(2)}) copy-start(bf16[2,1024,512]{2,1,0:T(8,128)(2,1)} %param.26) | copy-start | bytes 6291460
  1375.5 199.4 %copy-start.57 = (f32[1024]{0:T(1024)S(1)}, f32[1024]{0:T(1024)}, u32[]{:S(2)}) copy-start(f32[1024]{0:T(1024)} %copy-done.56) | copy-start | bytes 12292
  1375.5 199.4 %copy-start.59 = (f32[1024]{0:T(1024)S(1)}, f32[1024]{0:T(1024)}, u32[]{:S(2)}) copy-start(f32[1024]{0:T(1024)} %copy-done.58) | copy-start | bytes 12292
  1375.5 199.3 %copy-start.63 = (f32[1024]{0:T(1024)S(1)}, f32[1024]{0:T(1024)}, u32[]{:S(2)}) copy-start(f32[1024]{0:T(1024)} %copy-done.62) | copy-start | bytes 12292
  1375.5 199.3 %copy-start.65 = (f32[1024]{0:T(1024)S(1)}, f32[1024]{0:T(1024)}, u32[]{:S(2)}) copy-start(f32[1024]{0:T(1024)} %copy-done.64) | copy-start | bytes 12292
  1418.5 220.7 %copy-start.49 = (f32[2,64,64]{2,1,0:T(8,128)}, f32[2,64,64]{2,1,0:T(8,128)S(1)}, u32[]{:S(2)}) copy-start(f32[2,64,64]{2,1,0:T(8,128)S(1)} %get-tuple-element.462) | copy-start | bytes 98308
  (126 other events, 1020.8 us)
Sparse Core Ops, SparseCore 0:
  13.9 37.1 all-gather.10
  53.2 34.4 all-gather.6
  258.5 72.3 reduce-scatter.18
  425.7 72.1 reduce-scatter.14
  503.8 55.9 all-gather.12
  561.2 51.2 all-gather.8
  652.5 64.1 reduce-scatter.34
  766.3 70.0 reduce-scatter.22
  839.1 71.3 reduce-scatter.26
  912.9 44.5 reduce-scatter.20
  960.0 44.5 reduce-scatter.16
  1013.2 34.4 all-gather.14
  1049.2 34.4 all-gather.16
  1086.9 64.2 reduce-scatter.32
  1353.2 62.1 reduce-scatter.36
  1418.6 63.1 reduce-scatter.30
  1484.2 43.6 reduce-scatter.24
  1530.2 44.5 reduce-scatter.28
